TPU v7x, 32 devices: a whole 2x2x4 slice. The times are simulated.
32 devices in a mesh: groups: 2 (over x), seq: 16 (over z, y, core).
Axes of the slice: x: 2, y: 2, z: 4, core: 2. Of those that a mesh axis runs over, the one named last changes fastest.
Arguments:
- signal: bfloat16 [16384, 2048], P(('groups', 'seq')), parts along dimension 0, may hold values from -6 to 6
- gate_input: bfloat16 [16384, 2048], P(('groups', 'seq')), parts along dimension 0, may hold values from -6 to 6
- cotangent: bfloat16 [16384, 2048], P(('groups', 'seq')), parts along dimension 0, may hold values from -6 to 6
- block_factor: bfloat16 [512, 512], replicated, may hold values from -0.25 to 0.25
- cross_factor: bfloat16 [512, 16, 16], P('seq'), may hold values from -1.5 to 1.5
- order_table: int32 [512], replicated, may hold values from 0 to 511, each once
Outputs:
- grad_signal: bfloat16 [16384, 2048], P(('groups', 'seq')), parts along dimension 0
- grad_gate: bfloat16 [16384, 2048], P(('groups', 'seq')), parts along dimension 0
- grad_block: float32 [1024, 512], P('groups'), parts along dimension 0
- grad_cross: float32 [512, 32, 16], P('seq', 'groups'), parts along dimension 1
There are 2 independent parts, one for each index of `groups`. A program takes and returns all parts, laid end to end along the dimension named above; an argument that names none is the same for every part. Nothing has to cross between parts.
Inputs may be any that keep to these rules, and one draw needn't show every extreme that they name: order_table holds every number of 0 to 511 exactly once.
All inputs are finite; a program needn't handle non-finite values.
Results may differ from a plain program's by a relative error of at most 0.0057.
Values may be sent and summed in bfloat16 or wider, within the bound.
A program may use at most 64 MiB of HBM per device.

v0:
```python
import math
import jax
import jax.numpy as jnp
from jax import lax
from jax.sharding import PartitionSpec as P


def per_device(signal, gate_input, cotangent, block_factor, cross_factor, order_table):
    f32 = jnp.float32
    bf16 = jnp.bfloat16
    count = lax.axis_size("seq")
    width = signal.shape[1]
    permuted = jnp.take(signal, order_table, axis=0)
    mixed = jnp.dot(block_factor, permuted, preferred_element_type=f32).astype(bf16)
    gate_grad = (cotangent.astype(f32) * gate_input.astype(f32)).astype(bf16)
    spread_mixed = lax.all_to_all(mixed[None], "seq", split_axis=1, concat_axis=0, tiled=True)
    spread_grad = lax.all_to_all(gate_grad[None], "seq", split_axis=1, concat_axis=0, tiled=True)
    gated = jnp.einsum(
        "cij,jcd->icd", cross_factor, spread_mixed, preferred_element_type=f32
    ).astype(bf16)
    gated_home = lax.all_to_all(gated, "seq", split_axis=0, concat_axis=1, tiled=True)
    grad_cross = jnp.einsum(
        "icd,jcd->cij", spread_grad, spread_mixed, preferred_element_type=f32
    ) / math.sqrt(width)
    back = jnp.einsum("cij,icd->jcd", cross_factor, spread_grad, preferred_element_type=f32).astype(
        bf16
    )
    back_home = lax.all_to_all(back, "seq", split_axis=0, concat_axis=1, tiled=True)
    grad_gate = (cotangent.astype(f32) * gated_home[0].astype(f32)).astype(bf16)
    back_rows = back_home[0]
    partial_block = lax.dot_general(
        back_rows, permuted, (((1,), (1,)), ((), ())), preferred_element_type=f32
    )
    grad_block = lax.psum(partial_block, "seq") / math.sqrt(count * width)
    spread = lax.dot_general(
        block_factor, back_rows, (((0,), (0,)), ((), ())), preferred_element_type=f32
    ).astype(bf16)
    grad_signal = jnp.zeros_like(spread).at[order_table].set(spread)
    return (grad_signal, grad_gate, grad_block, grad_cross)


def solution(mesh):
    in_specs = (
        P(("groups", "seq"), None),
        P(("groups", "seq"), None),
        P(("groups", "seq"), None),
        P(),
        P("seq", None, None),
        P(),
    )
    out_specs = (
        P(("groups", "seq"), None),
        P(("groups", "seq"), None),
        P("groups", None),
        P("seq", "groups", None),
    )
    return jax.shard_map(
        per_device, mesh=mesh, in_specs=in_specs, out_specs=out_specs, check_vma=False
    )
```

profile of v0, /device:TPU:0, one launch (start us, length us, event | category | flops | bytes accessed | tf_op | source)
XLA Modules:
  0.0 409.7 jit_solution(3647754906035799778)
XLA Ops:
  7.2 0.0 copy-start
  7.2 0.8 compare_and_fusion
  8.0 0.7 compare_select_fusion
  8.7 0.1 copy-done
  8.8 0.0 copy-start.10
  8.8 3.3 gather_fusion
  12.1 0.0 copy-done.10
  12.1 3.1 fusion.3
  15.1 7.7 %copy.32 = bf16[1,512,2048]{2,0,1:T(2,128)(2,1)} copy(bf16[1,512,2048]{1,2,0:T(8,128)(2,1)S(1)} %fusion.3) | data formatting | bytes 4194304 | tf_op jit(solution)/shard_map/broadcast_in_dim | solution.py:16
  22.9 0.5 broadcast.9
  23.4 13.2 %reduce = bf16[512,2048]{1,0:T(8,128)(2,1)S(1)} reduce(bf16[512,1,2048]{2,1,0:T(2,128)(2,1)} %bitcast.31, bf16[]{:T(256)} %broadcast.9), dimensions={1}, to_apply=%bitcast.20.reduce_sub_computation | reduce | bytes 4194306
  36.5 2.8 reshape.52
  39.3 0.0 copy-start.9
  39.3 7.5 %all-to-all-start.2 = ((bf16[16,2,32768]{2,1,0:T(2,128)(2,1)}), bf16[16,2,32768]{2,1,0:T(2,128)(2,1)S(1)}, u32[]{:S(2)}, u32[]{:S(2)}) async-start(bf16[16,2,32768]{2,1,0:T(2,128)(2,1)} %reshape.52), calls=%async_computation.2 | async-start | bytes 4194304 | tf_op jit(solution)/shard_map/all_to_all | solution.py:16
  46.8 0.0 all-reduce.2.cloned.1.call-start
  46.9 0.0 copy-done.9
  46.9 0.2 copy.34
  47.1 40.9 %all-to-all-done.2 = bf16[16,2,32768]{2,1,0:T(2,128)(2,1)S(1)} async-done(((bf16[16,2,32768]{2,1,0:T(2,128)(2,1)}), bf16[16,2,32768]{2,1,0:T(2,128)(2,1)S(1)}, u32[]{:S(2)}, u32[]{:S(2)}) %all-to-all-start.2) | async-done | bytes 2097184 | tf_op jit(solution)/shard_map/all_to_all | solution.py:16
  87.9 6.7 %reshape.53 = bf16[512,1,2048]{2,1,0:T(2,128)(2,1)} reshape(bf16[16,2,32768]{2,1,0:T(2,128)(2,1)S(1)} %all-to-all-done.2) | data formatting | bytes 4194304
  94.7 3.5 copy.40
  98.1 0.0 copy-start.2
  98.1 2.4 fusion.5
  100.6 0.0 copy-done.2
  100.6 1.2 copy.35
  101.7 0.0 copy-start.5
  101.8 0.0 copy-start.6
  101.8 58.6 %all_to_all.42 = bf16[16,32,2048]{2,1,0:T(8,128)(2,1)S(1)} all-to-all(bf16[16,32,2048]{2,1,0:T(8,128)(2,1)S(1)} %copy.35), channel_id=1, replica_groups=mesh['groups'=2,'seq'=16] {'seq'}, dimensions={0} | all-to-all | bytes 4194304 | tf_op jit(solution)/shard_map/all_to_all | solution.py:21
  160.4 0.0 copy-done.5
  160.4 0.0 copy-done.6
  160.4 3.0 fusion.1
  163.3 5.2 %copy.54 = bf16[1,512,2048]{2,0,1:T(2,128)(2,1)} copy(bf16[1,512,2048]{2,1,0:T(8,128)(2,1)S(1)} %get-tuple-element.17) | data formatting | bytes 4194304 | tf_op jit(solution)/shard_map/broadcast_in_dim | solution.py:17
  168.5 13.2 %reduce.1 = bf16[512,2048]{1,0:T(8,128)(2,1)S(1)} reduce(bf16[512,1,2048]{2,1,0:T(2,128)(2,1)} %bitcast.32, bf16[]{:T(256)} %broadcast.9), dimensions={1}, to_apply=%bitcast.29.reduce_sub_computation | reduce | bytes 4194306
  181.7 2.8 reshape.50
  184.4 52.4 %all_to_all.43 = bf16[16,2,32768]{2,1,0:T(2,128)(2,1)S(1)} all-to-all(bf16[16,2,32768]{2,1,0:T(2,128)(2,1)} %reshape.50), channel_id=1, replica_groups=mesh['groups'=2,'seq'=16] {'seq'}, dimensions={0} | all-to-all | bytes 4194304 | tf_op jit(solution)/shard_map/all_to_all | solution.py:17
  236.9 6.7 %reshape.51 = bf16[512,1,2048]{2,1,0:T(2,128)(2,1)} reshape(bf16[16,2,32768]{2,1,0:T(2,128)(2,1)S(1)} %all_to_all.43) | data formatting | bytes 4194304
  243.6 3.5 copy.39
  247.1 0.0 copy-start.4
  247.1 2.4 fusion.4
  249.5 0.0 copy-done.4
  249.5 1.2 copy.30
  250.6 0.0 copy-start.7
  250.7 52.4 %all_to_all.44 = bf16[16,32,2048]{2,1,0:T(8,128)(2,1)S(1)} all-to-all(bf16[16,32,2048]{2,1,0:T(8,128)(2,1)S(1)} %copy.30), channel_id=1, replica_groups=mesh['groups'=2,'seq'=16] {'seq'}, dimensions={0} | all-to-all | bytes 4194304 | tf_op jit(solution)/shard_map/all_to_all | solution.py:28
  303.0 0.0 copy-start.8
  303.0 1.4 copy-done.8
  304.4 0.0 copy-done.7
  304.4 0.0 copy-start.3
  304.4 2.3 fusion.19
  306.7 0.0 all-reduce.2.cloned.1.call-update
  306.7 0.0 copy-done.3
  306.7 3.9 fusion.12
  310.6 0.8 copy.38
  311.5 4.3 %fusion.2 = bf16[512,2048]{0,1:T(8,128)(2,1)} fusion(bf16[512,2048]{1,0:T(8,128)(2,1)} %bitcast.40, bf16[512,512]{1,0:T(8,128)(2,1)S(1)} %copy-done.10), kind=kOutput, calls=%fused_computation.10 | convolution fusion | flops 1074790400 | bytes 4718592 | tf_op jit(solution)/shard_map/dot_general | solution.py:35
  315.8 0.0 copy-start.1
  315.8 4.1 %copy.31 = bf16[512,2048]{1,0:T(8,128)(2,1)} copy(bf16[512,2048]{0,1:T(8,128)(2,1)} %fusion.2) | data formatting | bytes 4194304 | tf_op jit(solution)/shard_map/convert_element_type | solution.py:37
  319.9 6.1 %scatter_custom_fusion = bf16[512,2048]{1,0:T(8,128)(2,1)} fusion(s32[512]{0:T(512)S(1)} %compare_select_fusion, bf16[512,2048]{1,0:T(8,128)(2,1)} %copy.31, bf16[]{:T(256)} %constant.8.clone.1), kind=kCustom, calls=%fused_computation.22 | custom fusion | bytes 2097664 | tf_op jit(solution)/shard_map/scatter | solution.py:38
  326.0 74.5 %all-reduce.2.cloned.1.call-done = f32[512,512]{1,0:T(8,128)} async-done(((f32[512,512]{1,0:T(8,128)}), f32[512,512]{1,0:T(8,128)}) %all-reduce.2.cloned.1.call-update) | async-done | bytes 1048592 | tf_op jit(solution)/shard_map/psum | solution.py:34
  400.6 2.3 broadcast_multiply_fusion
  402.9 0.0 copy-done.1
  (1 shorter events, 0.0 us)
Async XLA Ops:
  7.2 1.6 copy-start
  8.8 3.3 copy-start.10
  39.3 7.6 %copy-start.9 = (bf16[32,16,16]{0,2,1:T(8,128)(2,1)S(1)}, bf16[32,16,16]{0,2,1:T(8,128)(2,1)}, u32[]{:S(2)}) copy-start(bf16[32,16,16]{0,2,1:T(8,128)(2,1)} %param.10) | copy-start | bytes 49156
  39.3 48.6 %all-to-all-start.2 = ((bf16[16,2,32768]{2,1,0:T(2,128)(2,1)}), bf16[16,2,32768]{2,1,0:T(2,128)(2,1)S(1)}, u32[]{:S(2)}, u32[]{:S(2)}) async-start(bf16[16,2,32768]{2,1,0:T(2,128)(2,1)} %reshape.52), calls=%async_computation.2 | async-start | bytes 4194304 | tf_op jit(solution)/shard_map/all_to_all | solution.py:16
  46.8 353.7 %all-reduce.2.cloned.1.call-start = ((), (), s32[]{:S(2)}) async-start(), calls=%async_computation.4 | async-start | bytes 2097152 | tf_op jit(solution)/shard_map/psum | solution.py:34
  98.1 2.4 copy-start.2
  101.7 58.6 %copy-start.5 = (bf16[512,2048]{1,0:T(8,128)(2,1)S(1)}, bf16[512,2048]{1,0:T(8,128)(2,1)}, u32[]{:S(2)}) copy-start(bf16[512,2048]{1,0:T(8,128)(2,1)} %param.8) | copy-start | bytes 6291460
  101.8 58.6 %copy-start.6 = (bf16[512,2048]{1,0:T(8,128)(2,1)S(1)}, bf16[512,2048]{1,0:T(8,128)(2,1)}, u32[]{:S(2)}) copy-start(bf16[512,2048]{1,0:T(8,128)(2,1)} %param.7) | copy-start | bytes 6291460
  247.1 2.4 copy-start.4
  250.6 53.7 %copy-start.7 = (bf16[512,2048]{1,0:T(8,128)(2,1)S(1)}, bf16[512,2048]{1,0:T(8,128)(2,1)}, u32[]{:S(2)}) copy-start(bf16[512,2048]{1,0:T(8,128)(2,1)} %gather_fusion) | copy-start | bytes 6291460
  303.0 1.4 copy-start.8
  304.4 2.4 copy-start.3
  315.8 87.1 %copy-start.1 = (bf16[512,2048]{1,0:T(8,128)(2,1)S(1)}, bf16[512,2048]{1,0:T(8,128)(2,1)}, u32[]{:S(2)}) copy-start(bf16[512,2048]{1,0:T(8,128)(2,1)} %param.6) | copy-start | bytes 6291460
Sparse Core Ops, SparseCore 0:
  306.9 93.6 all-reduce.1
where the time goes:
time: 410 us
  blocking collectives  163 us (40%)
  waiting for transfers between devices  115 us (28%)
  local copies, waits for them, and re-layouts  57.6 us (14%)
  other arithmetic  33.1 us (8%)
  matrix products  18.5 us (5%)
  between operations  14.2 us (3%)
  starting transfers between devices  7.56 us (2%)
    psum x1, waiting for transfers between devices, per_device(): grad_block = lax.psum(partial_block, 'seq') / math.sqrt(count * width)  74.5 us
    all_to_all x1, blocking collectives, per_device(): lax.all_to_all(gated, 'seq', split_axis=0, concat_axis=1, tiled=True)  58.6 us
    all_to_all x1, blocking collectives, per_device(): lax.all_to_all(gate_grad[None], 'seq', split_axis=1, concat_axis=0, tiled...  52.4 us
    all_to_all x1, blocking collectives, per_device(): lax.all_to_all(back, 'seq', split_axis=0, concat_axis=1, tiled=True)  52.4 us
    all_to_all x1, waiting for transfers between devices, per_device(): lax.all_to_all(mixed[None], 'seq', split_axis=1, concat_axis=0, tiled=True)  40.9 us
    unnamed x31, local copies, waits for them, and re-layouts  28.9 us
    unnamed x2, other arithmetic  26.3 us
  transfers between devices with their start and end apart: 2, of which 2 were waited for; matrix products, arithmetic and copies ran while one was open for 5% of the time, Pallas kernels for 0%

commit v1 on v0

--- a/solution.py
+++ b/solution.py
@@ -3,6 +3,10 @@
 import jax.numpy as jnp
 from jax import lax
 from jax.sharding import PartitionSpec as P
+
+
+def _mark_patches(raw, row_axis):
+    return jnp.sum(lax.all_gather(raw, row_axis), axis=0)
 
 
 def per_device(signal, gate_input, cotangent, block_factor, cross_factor, order_table):
@@ -31,7 +35,7 @@
     partial_block = lax.dot_general(
         back_rows, permuted, (((1,), (1,)), ((), ())), preferred_element_type=f32
     )
-    grad_block = lax.psum(partial_block, "seq") / math.sqrt(count * width)
+    grad_block = _mark_patches(partial_block, row_axis="seq") / math.sqrt(count * width)
     spread = lax.dot_general(
         block_factor, back_rows, (((0,), (0,)), ((), ())), preferred_element_type=f32
     ).astype(bf16)

time: 410 us -> 467 us (1.14); the launches traced: 410 us -> 459 us
  waiting for transfers between devices: 115 us -> 151 us
  blocking collectives: 163 us -> 172 us
  other arithmetic: 33.1 us -> 39.9 us
    all_gather x0 -> x1, waiting for transfers between devices: none -> 110 us  [_mark_patches(): return jnp.sum(lax.all_gather(raw, row_axis), axis=0)]
    psum x1 -> x0, waiting for transfers between devices: 74.5 us -> none  [per_device(): grad_block = lax.psum(partial_block, 'seq') / math.sqrt(count * width)]
    all_to_all x1, blocking collectives: 52.4 us -> 60.7 us  [per_device(): lax.all_to_all(back, 'seq', split_axis=0, concat_axis=1, tiled=True)]
    reduce_sum x0 -> x1, other arithmetic: none -> 8.05 us  [_mark_patches(): return jnp.sum(lax.all_gather(raw, row_axis), axis=0)]
  transfers between devices with their start and end apart: 2 -> 2, of which waited for: 2 -> 2; matrix products, arithmetic and copies ran while one was open for 5% -> 4% of each run, Pallas kernels for 0% -> 0%
where the time goes in v1:
time: 467 us; the launch traced here: 459 us
  blocking collectives  172 us (37%)
  waiting for transfers between devices  151 us (32%)
  local copies, waits for them, and re-layouts  55.4 us (12%)
  other arithmetic  39.9 us (9%)
  matrix products  18.4 us (4%)
  between operations  14.2 us (3%)
  starting transfers between devices  7.56 us (2%)
    all_gather x1, waiting for transfers between devices, _mark_patches(): return jnp.sum(lax.all_gather(raw, row_axis), axis=0)  110 us
    all_to_all x1, blocking collectives, per_device(): lax.all_to_all(back, 'seq', split_axis=0, concat_axis=1, tiled=True)  60.7 us
    all_to_all x1, blocking collectives, per_device(): lax.all_to_all(gated, 'seq', split_axis=0, concat_axis=1, tiled=True)  58.9 us
    all_to_all x1, blocking collectives, per_device(): lax.all_to_all(gate_grad[None], 'seq', split_axis=1, concat_axis=0, tiled...  52.4 us
    all_to_all x1, waiting for transfers between devices, per_device(): lax.all_to_all(mixed[None], 'seq', split_axis=1, concat_axis=0, tiled=True)  40.9 us
    unnamed x31, local copies, waits for them, and re-layouts  28.8 us
    unnamed x2, other arithmetic  26.3 us
  transfers between devices with their start and end apart: 2, of which 2 were waited for; matrix products, arithmetic and copies ran while one was open for 4% of the time, Pallas kernels for 0%

profile of v1, /device:TPU:0, one launch (start us, length us, event | category | flops | bytes accessed | tf_op | source)
XLA Modules:
  0.0 458.8 jit_solution(8575304290987735815)
XLA Ops:
  7.2 0.0 copy-start
  7.2 0.8 compare_and_fusion
  8.0 0.7 compare_select_fusion
  8.7 0.1 copy-done
  8.8 0.0 copy-start.10
  8.8 3.3 gather_fusion
  12.1 0.0 copy-done.10
  12.1 3.1 fusion.3
  15.1 7.7 %copy.32 = bf16[1,512,2048]{2,0,1:T(2,128)(2,1)} copy(bf16[1,512,2048]{1,2,0:T(8,128)(2,1)S(1)} %fusion.3) | data formatting | bytes 4194304 | tf_op jit(solution)/shard_map/broadcast_in_dim | solution.py:20
  22.9 0.5 broadcast.9
  23.4 13.2 %reduce = bf16[512,2048]{1,0:T(8,128)(2,1)S(1)} reduce(bf16[512,1,2048]{2,1,0:T(2,128)(2,1)} %bitcast.33, bf16[]{:T(256)} %broadcast.9), dimensions={1}, to_apply=%bitcast.21.reduce_sub_computation | reduce | bytes 4194306
  36.5 2.8 reshape.53
  39.3 0.0 copy-start.9
  39.3 7.5 %all-to-all-start.2 = ((bf16[16,2,32768]{2,1,0:T(2,128)(2,1)}), bf16[16,2,32768]{2,1,0:T(2,128)(2,1)S(1)}, u32[]{:S(2)}, u32[]{:S(2)}) async-start(bf16[16,2,32768]{2,1,0:T(2,128)(2,1)} %reshape.53), calls=%async_computation.2 | async-start | bytes 4194304 | tf_op jit(solution)/shard_map/all_to_all | solution.py:20
  46.8 0.0 all-gather.3.cloned.1.call-start
  46.9 0.0 copy-done.9
  46.9 0.2 copy.34
  47.1 40.9 %all-to-all-done.2 = bf16[16,2,32768]{2,1,0:T(2,128)(2,1)S(1)} async-done(((bf16[16,2,32768]{2,1,0:T(2,128)(2,1)}), bf16[16,2,32768]{2,1,0:T(2,128)(2,1)S(1)}, u32[]{:S(2)}, u32[]{:S(2)}) %all-to-all-start.2) | async-done | bytes 2097184 | tf_op jit(solution)/shard_map/all_to_all | solution.py:20
  87.9 6.7 %reshape.54 = bf16[512,1,2048]{2,1,0:T(2,128)(2,1)} reshape(bf16[16,2,32768]{2,1,0:T(2,128)(2,1)S(1)} %all-to-all-done.2) | data formatting | bytes 4194304
  94.7 3.5 copy.40
  98.1 0.0 copy-start.2
  98.1 2.4 fusion.5
  100.6 0.0 copy-done.2
  100.6 1.2 copy.35
  101.7 0.0 copy-start.5
  101.8 0.0 copy-start.6
  101.8 58.9 %all_to_all.42 = bf16[16,32,2048]{2,1,0:T(8,128)(2,1)S(1)} all-to-all(bf16[16,32,2048]{2,1,0:T(8,128)(2,1)S(1)} %copy.35), channel_id=1, replica_groups=mesh['groups'=2,'seq'=16] {'seq'}, dimensions={0} | all-to-all | bytes 4194304 | tf_op jit(solution)/shard_map/all_to_all | solution.py:25
  160.7 0.0 copy-done.5
  160.7 0.0 copy-done.6
  160.7 3.0 fusion.1
  163.6 5.2 %copy.54 = bf16[1,512,2048]{2,0,1:T(2,128)(2,1)} copy(bf16[1,512,2048]{2,1,0:T(8,128)(2,1)S(1)} %get-tuple-element.17) | data formatting | bytes 4194304 | tf_op jit(solution)/shard_map/broadcast_in_dim | solution.py:21
  168.8 13.2 %reduce.1 = bf16[512,2048]{1,0:T(8,128)(2,1)S(1)} reduce(bf16[512,1,2048]{2,1,0:T(2,128)(2,1)} %bitcast.34, bf16[]{:T(256)} %broadcast.9), dimensions={1}, to_apply=%bitcast.30.reduce_sub_computation | reduce | bytes 4194306
  182.0 2.8 reshape.51
  184.8 52.4 %all_to_all.43 = bf16[16,2,32768]{2,1,0:T(2,128)(2,1)S(1)} all-to-all(bf16[16,2,32768]{2,1,0:T(2,128)(2,1)} %reshape.51), channel_id=1, replica_groups=mesh['groups'=2,'seq'=16] {'seq'}, dimensions={0} | all-to-all | bytes 4194304 | tf_op jit(solution)/shard_map/all_to_all | solution.py:21
  237.2 6.7 %reshape.52 = bf16[512,1,2048]{2,1,0:T(2,128)(2,1)} reshape(bf16[16,2,32768]{2,1,0:T(2,128)(2,1)S(1)} %all_to_all.43) | data formatting | bytes 4194304
  243.9 3.5 copy.39
  247.4 0.0 copy-start.4
  247.4 2.4 fusion.4
  249.8 0.0 copy-done.4
  249.8 1.2 copy.30
  250.9 0.0 copy-start.7
  251.0 60.7 %all_to_all.44 = bf16[16,32,2048]{2,1,0:T(8,128)(2,1)S(1)} all-to-all(bf16[16,32,2048]{2,1,0:T(8,128)(2,1)S(1)} %copy.30), channel_id=1, replica_groups=mesh['groups'=2,'seq'=16] {'seq'}, dimensions={0} | all-to-all | bytes 4194304 | tf_op jit(solution)/shard_map/all_to_all | solution.py:32
  311.7 0.0 copy-start.8
  311.7 1.3 copy-done.8
  313.0 0.0 copy-done.7
  313.0 0.0 copy-start.3
  313.0 2.3 fusion.19
  315.3 0.0 all-gather.3.cloned.1.call-update
  315.3 0.0 copy-done.3
  315.3 3.9 fusion.12
  319.2 0.8 copy.38
  320.1 4.2 fusion.2
  324.3 3.0 copy.31
  327.3 5.1 %scatter_custom_fusion = bf16[512,2048]{1,0:T(8,128)(2,1)} fusion(s32[512]{0:T(512)S(1)} %compare_select_fusion, bf16[512,2048]{1,0:T(8,128)(2,1)S(1)} %copy.31, bf16[]{:T(256)} %constant.8.clone.1), kind=kCustom, calls=%fused_computation.22 | custom fusion | bytes 2097154 | tf_op jit(solution)/shard_map/scatter | solution.py:42
  332.4 110.4 %all-gather.3.cloned.1.call-done = f32[8192,512]{1,0:T(8,128)} async-done(((f32[512,512]{1,0:T(8,128)}), f32[8192,512]{1,0:T(8,128)}) %all-gather.3.cloned.1.call-update) | async-done | bytes 16777232 | tf_op jit(solution)/shard_map/all_gather | solution.py:9
  442.8 0.0 copy-start.1
  442.8 8.1 %reduce_sum.9 = f32[512,512]{1,0:T(8,128)S(1)} reduce(f32[16,512,512]{2,1,0:T(8,128)} %bitcast.32, f32[]{:T(128)} %constant.25.clone.1), dimensions={0}, to_apply=%region_1.2 | reduce | flops 3932160 | bytes 17825796 | tf_op jit(solution)/shard_map/reduce_sum | solution.py:9
  450.8 1.1 broadcast_multiply_fusion
  451.9 0.0 copy-done.1
  (1 shorter events, 0.0 us)
Async XLA Ops:
  7.2 1.6 copy-start
  8.8 3.3 copy-start.10
  39.3 7.6 %copy-start.9 = (bf16[32,16,16]{0,2,1:T(8,128)(2,1)S(1)}, bf16[32,16,16]{0,2,1:T(8,128)(2,1)}, u32[]{:S(2)}) copy-start(bf16[32,16,16]{0,2,1:T(8,128)(2,1)} %param.10) | copy-start | bytes 49156
  39.3 48.6 %all-to-all-start.2 = ((bf16[16,2,32768]{2,1,0:T(2,128)(2,1)}), bf16[16,2,32768]{2,1,0:T(2,128)(2,1)S(1)}, u32[]{:S(2)}, u32[]{:S(2)}) async-start(bf16[16,2,32768]{2,1,0:T(2,128)(2,1)} %reshape.53), calls=%async_computation.2 | async-start | bytes 4194304 | tf_op jit(solution)/shard_map/all_to_all | solution.py:20
  46.8 396.0 %all-gather.3.cloned.1.call-start = ((), (), s32[]{:S(2)}) async-start(), calls=%async_computation.4 | async-start | bytes 17825792 | tf_op jit(solution)/shard_map/all_gather | solution.py:9
  98.1 2.4 copy-start.2
  101.7 58.9 %copy-start.5 = (bf16[512,2048]{1,0:T(8,128)(2,1)S(1)}, bf16[512,2048]{1,0:T(8,128)(2,1)}, u32[]{:S(2)}) copy-start(bf16[512,2048]{1,0:T(8,128)(2,1)} %param.8) | copy-start | bytes 6291460
  101.8 58.9 %copy-start.6 = (bf16[512,2048]{1,0:T(8,128)(2,1)S(1)}, bf16[512,2048]{1,0:T(8,128)(2,1)}, u32[]{:S(2)}) copy-start(bf16[512,2048]{1,0:T(8,128)(2,1)} %param.7) | copy-start | bytes 6291460
  247.4 2.4 copy-start.4
  250.9 62.0 %copy-start.7 = (bf16[512,2048]{1,0:T(8,128)(2,1)S(1)}, bf16[512,2048]{1,0:T(8,128)(2,1)}, u32[]{:S(2)}) copy-start(bf16[512,2048]{1,0:T(8,128)(2,1)} %gather_fusion) | copy-start | bytes 6291460
  311.7 1.3 copy-start.8
  313.0 2.4 copy-start.3
  442.8 9.1 %copy-start.1 = (bf16[512,2048]{1,0:T(8,128)(2,1)S(1)}, bf16[512,2048]{1,0:T(8,128)(2,1)}, u32[]{:S(2)}) copy-start(bf16[512,2048]{1,0:T(8,128)(2,1)} %param.6) | copy-start | bytes 6291460
Sparse Core Ops, SparseCore 0:
  315.5 127.2 all-gather.2
